TPU v7x, 32 devices: a whole 2x2x4 slice. The times are simulated.
32 devices in a mesh: srv: 2 (over y), blk: 8 (over z, x), rep: 2 (over core).
Axes of the slice: x: 2, y: 2, z: 4, core: 2. Of those that a mesh axis runs over, the one named last changes fastest.
Arguments:
- queries: bfloat16 [2, 8, 32, 4096], P('srv', 'blk', 'rep'), parts along dimension 2, may hold values from -16 to 16
- destination: int32 [2, 8, 8], P('srv', 'blk', 'rep'), parts along dimension 2, may hold values from 0 to 1, as said below
- offsets: int32 [2, 8, 8], P('srv', 'blk', 'rep'), parts along dimension 2, may hold values from 0 to 124
- key_rows: bfloat16 [2, 1024, 512], P('srv', 'blk', 'rep'), parts along dimension 2, may hold values from -16 to 16
- value_rows: bfloat16 [2, 1024, 512], P('srv', 'blk', 'rep'), parts along dimension 2, may hold values from -6 to 6
- lengths: int32 [2, 16], P('srv', 'rep'), parts along dimension 1, may hold values from 1 to 385, 1024 in all within a row
Outputs:
- attended: bfloat16 [2, 8, 32, 4096], P('srv', 'blk', 'rep'), parts along dimension 2
There are 2 independent parts, one for each index of `rep`. A program takes and returns all parts, laid end to end along the dimension named above; each array names one. Nothing has to cross between parts.
Inputs may be any that keep to these rules, and one draw needn't show every extreme that they name: `destination`: within each round (tasks r * 2 to r * 2 + 1 of a device) a device names 2 different servers; in each round and for each blk index, 2 servers are named by every device of that blk index.
All inputs are finite; a program needn't handle non-finite values.
Results may differ from a plain program's by a relative error of at most 0.0033.
Values may be sent and summed in bfloat16 or wider, within the bound.
A program may use at most 64 MiB of HBM per device.

v0:
```python
import math

import jax
import jax.numpy as jnp
from jax import lax
from jax.sharding import PartitionSpec as P

QH = 32
KVH = 2
HD = 128
R = 4
ROUNDS = 2


def from_behind(shard, axis, by):
    peers = lax.axis_size(axis)
    pairs = [(i, i + by) for i in range(peers) if 0 <= i + by < peers]
    return lax.ppermute(shard, axis, pairs)


def for_sending(shard):
    return jax.tree.map(lambda a: a.astype(jnp.bfloat16) if a.dtype == jnp.float32 else a, shard)


def document_of(positions, boundary):
    return jnp.sum((boundary[None, :] <= positions[:, None]).astype(jnp.int32), axis=1)


def give_back(served):
    return lax.all_to_all(served, "srv", split_axis=0, concat_axis=0, tiled=True)


def on_device(queries, destination, offsets, key_rows, value_rows, lengths):
    servers = lax.axis_size("srv")
    blk_index = lax.axis_index("blk")
    block_rows = key_rows.shape[1]
    kv_width = key_rows.shape[2]
    query_width = queries.shape[3]
    per_round = destination.shape[2] // ROUNDS
    groups = QH // KVH
    scaling = 1.0 / math.sqrt(HD)
    boundary = jnp.cumsum(lengths[0])
    joined = jnp.concatenate([key_rows[0], value_rows[0]], axis=1)
    pieces = [joined]
    current = joined
    for hop_number in range(3):
        current = from_behind(current, "blk", 1)
        pieces.append(current)
    window = jnp.concatenate(pieces[::-1], axis=0)
    key_pos = (blk_index - 3) * block_rows + jnp.arange(4 * block_rows, dtype=jnp.int32)
    key_valid = key_pos >= 0
    key_doc = document_of(key_pos, boundary)
    key_heads = jnp.transpose(window[:, :kv_width].reshape(4 * block_rows, KVH, HD), (1, 0, 2))
    value_heads = jnp.transpose(window[:, kv_width:].reshape(4 * block_rows, KVH, HD), (1, 0, 2))
    local_queries = queries[0, 0].reshape(ROUNDS, per_round, R, query_width)
    local_targets = destination[0, 0].reshape(ROUNDS, per_round)
    local_starts = offsets[0, 0].reshape(ROUNDS, per_round)
    outgoing = []
    for turn in range(ROUNDS):
        sending = (
            jnp.zeros((servers, 1, R, query_width), jnp.bfloat16)
            .at[local_targets[turn], 0]
            .set(local_queries[turn])
        )
        placing = (
            jnp.zeros((servers, 1), jnp.int32).at[local_targets[turn], 0].set(local_starts[turn])
        )
        outgoing.append((sending, placing))
    collected = []
    for turn in range(ROUNDS):
        query_buffer, offset_buffer = lax.all_to_all(
            for_sending(outgoing[turn]), "srv", split_axis=0, concat_axis=0, tiled=True
        )
        leading = query_buffer.shape[:2]
        rows = query_buffer.reshape(-1, query_width)
        query_pos = (
            blk_index * block_rows + offset_buffer[..., None] + jnp.arange(R, dtype=jnp.int32)
        )
        query_pos = query_pos.reshape(-1)
        query_doc = document_of(query_pos, boundary)
        allowed = (
            key_valid[None, :]
            & (key_pos[None, :] <= query_pos[:, None])
            & (key_doc[None, :] == query_doc[:, None])
        )
        query_heads = jnp.transpose(rows.reshape(-1, KVH, groups, HD), (1, 0, 2, 3))

        def one_head(triple):
            query_head, key_head, value_head = triple
            scores = (
                jnp.einsum("mgd,nd->gmn", query_head, key_head, preferred_element_type=jnp.float32)
                * scaling
            )
            scores = jnp.where(allowed[None], scores, -1e30)
            highest = jnp.max(scores, axis=2, keepdims=True)
            weights = jnp.exp(scores - highest)
            denominator = jnp.sum(weights, axis=2)
            weighted = jnp.einsum(
                "gmn,nd->mgd",
                weights.astype(jnp.bfloat16),
                value_head,
                preferred_element_type=jnp.float32,
            )
            return weighted / jnp.transpose(denominator)[:, :, None]

        per_head = lax.map(one_head, (query_heads, key_heads, value_heads))
        merged = jnp.transpose(per_head, (1, 0, 2, 3)).reshape(rows.shape).astype(jnp.bfloat16)
        served = merged.reshape(leading + (R, query_width))
        returned = give_back(served)
        collected.append(returned[local_targets[turn], 0])
    gathered = jnp.stack(collected)
    return gathered.reshape(1, 1, ROUNDS * per_round * R, query_width)


def solution(mesh):
    placed = (
        P("srv", "blk", "rep", None),
        P("srv", "blk", "rep"),
        P("srv", "blk", "rep"),
        P("srv", "blk", "rep"),
        P("srv", "blk", "rep"),
        P("srv", "rep"),
    )
    return jax.shard_map(
        on_device,
        mesh=mesh,
        in_specs=placed,
        out_specs=P("srv", "blk", "rep", None),
        check_vma=False,
    )
```

profile of v0, /device:TPU:0, one launch (start us, length us, event | category | flops | bytes accessed | tf_op | source)
XLA Modules:
  0.0 65.8 jit_solution(7263073896091319962)
XLA Ops:
  0.0 0.8 %shift-left_bitcast_fusion.1 = (s32[2]{0:T(128)S(1)}, s32[2]{0:T(128)S(1)}, s32[2]{0:T(128)S(1)}, s32[2]{0:T(128)S(1)}) fusion(s32[1,1,4]{2,1,0:T(1,128)} %param.11), kind=kLoop, calls=%fused_computation.65 | loop fusion | flops 20 | bytes 48 | tf_op jit(solution)/shard_map/concatenate | solution.py:63
  2.1 4.3 %all-to-all-start = ((s32[2,1,1]{2,1,0:T(1,128)}), s32[2,1,1]{2,1,0:T(1,128)S(1)}, u32[]{:S(2)}, u32[]{:S(2)}) async-start(s32[2,1,1]{2,1,0:T(1,128)} %copy.49), calls=%async_computation | async-start | bytes 2048 | tf_op jit(solution)/shard_map/all_to_all | solution.py:71
  6.4 1.0 %copy.47 = bf16[1,128,256]{1,2,0:T(8,128)(2,1)S(1)} copy(bf16[1,128,256]{2,1,0:T(8,128)(2,1)} %param.13) | data formatting | bytes 131072 | tf_op args[3]
  7.5 3.9 %collective-permute-start = (bf16[128,512]{0,1:T(8,128)(2,1)S(1)}, bf16[128,512]{0,1:T(8,128)(2,1)S(1)}, u32[]{:S(2)}, u32[]{:S(2)}) collective-permute-start(bf16[128,512]{0,1:T(8,128)(2,1)S(1)} %pad_maximum_fusion), channel_id=1, source_target_pairs={{0,2},{2,4},{4,6},{6,8},{8,10},{10,12},{12,14},{1,3},{3,5},{5,7},{... | collective-permute-start | bytes 393224 | tf_op jit(solution)/shard_map/ppermute | solution.py:18
  11.5 0.6 copy-done.3
  13.2 0.6 broadcast.142.clone.1
  13.8 2.0 %scatter_fusion = bf16[2,4,4096]{2,1,0:T(4,128)(2,1)} fusion(bf16[2,4,4096]{2,1,0:T(4,128)(2,1)} %broadcast.142.clone.1, s32[2]{0:T(128)S(1)} %get-tuple-element.257, bf16[2,4,4096]{2,1,0:T(4,128)(2,1)S(1)} %reshape.232), kind=kCustom, calls=%fused_computation.3 | custom fusion | bytes 196616 | tf_op jit(solution)/shard_map/scatter | solution.py:63
  16.4 2.0 %scatter_fusion.1 = bf16[2,4,4096]{2,1,0:T(4,128)(2,1)} fusion(bf16[2,4,4096]{2,1,0:T(4,128)(2,1)} %broadcast.142.clone, s32[2]{0:T(128)S(1)} %get-tuple-element.256, bf16[2,4,4096]{2,1,0:T(4,128)(2,1)S(1)} %reshape.252), kind=kCustom, calls=%fused_computation.5 | custom fusion | bytes 196616 | tf_op jit(solution)/shard_map/scatter | solution.py:63
  18.4 6.8 %all_to_all.38 = s32[2,1,1]{2,1,0:T(1,128)S(1)} all-to-all(s32[2,1,1]{2,1,0:T(1,128)S(1)} %copy.56), channel_id=1, replica_groups=mesh['srv'=2,'blk'=8,'rep'=2] {'srv'}, dimensions={0} | all-to-all | bytes 16 | tf_op jit(solution)/shard_map/all_to_all | solution.py:71
  25.2 3.3 %all-to-all-start.1 = ((bf16[2,1,4,4096]{3,2,1,0:T(4,128)(2,1)}), bf16[2,1,4,4096]{3,2,1,0:T(4,128)(2,1)S(1)}, u32[]{:S(2)}, u32[]{:S(2)}) async-start(bf16[2,1,4,4096]{3,2,1,0:T(4,128)(2,1)} %bitcast.8), calls=%async_computation.1 | async-start | bytes 131072 | tf_op jit(solution)/shard_map/all_to_all | solution.py:71
  28.7 3.5 %collective-permute-start.1 = (bf16[128,512]{0,1:T(8,128)(2,1)S(1)}, bf16[128,512]{0,1:T(8,128)(2,1)S(1)}, u32[]{:S(2)}, u32[]{:S(2)}) collective-permute-start(bf16[128,512]{0,1:T(8,128)(2,1)S(1)} %collective-permute-done), channel_id=1, source_target_pairs={{0,2},{2,4},{4,6},{6,8},{8,10},{10,12},{12,14},{1,3},{3,5},{5,7},{... | collective-permute-start | bytes 393224 | tf_op jit(solution)/shard_map/ppermute | solution.py:18
  32.2 2.4 %collective-permute-done.1 = bf16[128,512]{0,1:T(8,128)(2,1)S(1)} collective-permute-done((bf16[128,512]{0,1:T(8,128)(2,1)S(1)}, bf16[128,512]{0,1:T(8,128)(2,1)S(1)}, u32[]{:S(2)}, u32[]{:S(2)}) %collective-permute-start.1) | collective-permute-done | bytes 131104 | tf_op jit(solution)/shard_map/ppermute | solution.py:18
  34.6 4.3 %collective-permute-start.2 = (bf16[128,512]{0,1:T(8,128)(2,1)S(1)}, bf16[128,512]{0,1:T(8,128)(2,1)S(1)}, u32[]{:S(2)}, u32[]{:S(2)}) collective-permute-start(bf16[128,512]{0,1:T(8,128)(2,1)S(1)} %collective-permute-done.1), channel_id=1, source_target_pairs={{0,2},{2,4},{4,6},{6,8},{8,10},{10,12},{12,14},{1,3},{3,5},{5,7},{... | collective-permute-start | bytes 393224 | tf_op jit(solution)/shard_map/ppermute | solution.py:18
  39.2 3.3 %all-to-all-start.4 = ((bf16[2,1,4,4096]{3,2,1,0:T(4,128)(2,1)}), bf16[2,1,4,4096]{3,2,1,0:T(4,128)(2,1)S(1)}, u32[]{:S(2)}, u32[]{:S(2)}) async-start(bf16[2,1,4,4096]{3,2,1,0:T(4,128)(2,1)} %bitcast.23), calls=%async_computation.4 | async-start | bytes 131072 | tf_op jit(solution)/shard_map/all_to_all | solution.py:71
  42.8 3.8 %all-to-all-done.4 = bf16[2,1,4,4096]{3,2,1,0:T(4,128)(2,1)S(1)} async-done(((bf16[2,1,4,4096]{3,2,1,0:T(4,128)(2,1)}), bf16[2,1,4,4096]{3,2,1,0:T(4,128)(2,1)S(1)}, u32[]{:S(2)}, u32[]{:S(2)}) %all-to-all-start.4) | async-done | bytes 65568 | tf_op jit(solution)/shard_map/all_to_all | solution.py:71
  47.2 1.7 %while.22 = (s32[]{:T(128)}, bf16[2,8,16,128]{3,2,1,0:T(8,128)(2,1)S(1)}, bf16[2,512,128]{2,1,0:T(8,128)(2,1)S(1)}, bf16[2,512,128]{2,1,0:T(8,128)(2,1)S(1)}, bf...) while((s32[]{:T(128)}, ...), condition=%wide.region_8.9_spmd.clone, body=%wide.region_5.0_spmd.clone.sunk | while | flops 34045696 | bytes 1171629 | solution.py:106
  48.9 0.6 convert_element_type.51
  49.5 3.3 %all-to-all-start.2 = ((bf16[2,1,4,4096]{3,2,1,0:T(4,128)(2,1)}), bf16[2,1,4,4096]{3,2,1,0:T(4,128)(2,1)S(1)}, u32[]{:S(2)}, u32[]{:S(2)}) async-start(bf16[2,1,4,4096]{3,2,1,0:T(4,128)(2,1)} %bitcast.15), calls=%async_computation.2 | async-start | bytes 131072 | tf_op jit(solution)/shard_map/all_to_all | solution.py:30
  52.9 1.6 %while.23 = (s32[]{:T(128)}, bf16[2,8,16,128]{3,2,1,0:T(8,128)(2,1)S(1)}, bf16[2,512,128]{2,1,0:T(8,128)(2,1)S(1)}, bf16[2,512,128]{2,1,0:T(8,128)(2,1)S(1)}, bf...) while((s32[]{:T(128)}, ...), condition=%wide.region_15.16_spmd.clone, body=%wide.region_12.15_spmd.clone.sunk | while | flops 34045696 | bytes 1171629 | solution.py:106
  54.5 0.7 convert_element_type.55
  55.2 1.8 %all-to-all-done.2 = bf16[2,1,4,4096]{3,2,1,0:T(4,128)(2,1)S(1)} async-done(((bf16[2,1,4,4096]{3,2,1,0:T(4,128)(2,1)}), bf16[2,1,4,4096]{3,2,1,0:T(4,128)(2,1)S(1)}, u32[]{:S(2)}, u32[]{:S(2)}) %all-to-all-start.2) | async-done | bytes 65568 | tf_op jit(solution)/shard_map/all_to_all | solution.py:30
  57.0 3.3 %all-to-all-start.5 = ((bf16[2,1,4,4096]{3,2,1,0:T(4,128)(2,1)}), bf16[2,1,4,4096]{3,2,1,0:T(4,128)(2,1)S(1)}, u32[]{:S(2)}, u32[]{:S(2)}) async-start(bf16[2,1,4,4096]{3,2,1,0:T(4,128)(2,1)} %bitcast.28), calls=%async_computation.5 | async-start | bytes 131072 | tf_op jit(solution)/shard_map/all_to_all | solution.py:30
  60.9 3.5 %all-to-all-done.5 = bf16[2,1,4,4096]{3,2,1,0:T(4,128)(2,1)S(1)} async-done(((bf16[2,1,4,4096]{3,2,1,0:T(4,128)(2,1)}), bf16[2,1,4,4096]{3,2,1,0:T(4,128)(2,1)S(1)}, u32[]{:S(2)}, u32[]{:S(2)}) %all-to-all-start.5) | async-done | bytes 65568 | tf_op jit(solution)/shard_map/all_to_all | solution.py:30
  65.1 0.7 %reshape.203 = bf16[1,1,16,4096]{3,2,1,0:T(8,128)(2,1)} reshape(bf16[2,2,4,4096]{3,2,1,0:T(4,128)(2,1)S(1)} %pad_maximum_fusion.1) | data formatting | bytes 262144 | tf_op jit(solution)/shard_map/reshape | solution.py:112
  (61 shorter events, 8.9 us)
Async XLA Ops:
  0.0 0.8 %copy-start.2 = (s32[1,1,4]{2,1,0:T(1,128)S(1)}, s32[1,1,4]{2,1,0:T(1,128)}, u32[]{:S(2)}) copy-start(s32[1,1,4]{2,1,0:T(1,128)} %param.12) | copy-start | bytes 52
  2.1 16.3 %all-to-all-start = ((s32[2,1,1]{2,1,0:T(1,128)}), s32[2,1,1]{2,1,0:T(1,128)S(1)}, u32[]{:S(2)}, u32[]{:S(2)}) async-start(s32[2,1,1]{2,1,0:T(1,128)} %copy.49), calls=%async_computation | async-start | bytes 2048 | tf_op jit(solution)/shard_map/all_to_all | solution.py:71
  6.4 1.0 %copy-start.1 = (bf16[1,128,256]{2,1,0:T(8,128)(2,1)S(1)}, bf16[1,128,256]{2,1,0:T(8,128)(2,1)}, u32[]{:S(2)}) copy-start(bf16[1,128,256]{2,1,0:T(8,128)(2,1)} %param.14) | copy-start | bytes 196612
  7.5 4.8 %copy-start = (bf16[1,1,16,4096]{3,2,1,0:T(8,128)(2,1)S(1)}, bf16[1,1,16,4096]{3,2,1,0:T(8,128)(2,1)}, u32[]{:S(2)}) copy-start(bf16[1,1,16,4096]{3,2,1,0:T(8,128)(2,1)} %param.10) | copy-start | bytes 393220
  7.5 21.2 %collective-permute-start = (bf16[128,512]{0,1:T(8,128)(2,1)S(1)}, bf16[128,512]{0,1:T(8,128)(2,1)S(1)}, u32[]{:S(2)}, u32[]{:S(2)}) collective-permute-start(bf16[128,512]{0,1:T(8,128)(2,1)S(1)} %pad_maximum_fusion), channel_id=1, source_target_pairs={{0,2},{2,4},{4,6},{6,8},{8,10},{10,12},{12,14},{1,3},{3,5},{5,7},{... | collective-permute-start | bytes 393224 | tf_op jit(solution)/shard_map/ppermute | solution.py:18
  11.5 0.7 %copy-start.3 = (s32[1,8]{1,0:T(1,128)S(1)}, s32[1,8]{1,0:T(1,128)}, u32[]{:S(2)}) copy-start(s32[1,8]{1,0:T(1,128)} %param.15) | copy-start | bytes 100
  25.2 14.0 %all-to-all-start.1 = ((bf16[2,1,4,4096]{3,2,1,0:T(4,128)(2,1)}), bf16[2,1,4,4096]{3,2,1,0:T(4,128)(2,1)S(1)}, u32[]{:S(2)}, u32[]{:S(2)}) async-start(bf16[2,1,4,4096]{3,2,1,0:T(4,128)(2,1)} %bitcast.8), calls=%async_computation.1 | async-start | bytes 131072 | tf_op jit(solution)/shard_map/all_to_all | solution.py:71
  28.7 6.0 %collective-permute-start.1 = (bf16[128,512]{0,1:T(8,128)(2,1)S(1)}, bf16[128,512]{0,1:T(8,128)(2,1)S(1)}, u32[]{:S(2)}, u32[]{:S(2)}) collective-permute-start(bf16[128,512]{0,1:T(8,128)(2,1)S(1)} %collective-permute-done), channel_id=1, source_target_pairs={{0,2},{2,4},{4,6},{6,8},{8,10},{10,12},{12,14},{1,3},{3,5},{5,7},{... | collective-permute-start | bytes 393224 | tf_op jit(solution)/shard_map/ppermute | solution.py:18
  34.6 12.1 %collective-permute-start.2 = (bf16[128,512]{0,1:T(8,128)(2,1)S(1)}, bf16[128,512]{0,1:T(8,128)(2,1)S(1)}, u32[]{:S(2)}, u32[]{:S(2)}) collective-permute-start(bf16[128,512]{0,1:T(8,128)(2,1)S(1)} %collective-permute-done.1), channel_id=1, source_target_pairs={{0,2},{2,4},{4,6},{6,8},{8,10},{10,12},{12,14},{1,3},{3,5},{5,7},{... | collective-permute-start | bytes 393224 | tf_op jit(solution)/shard_map/ppermute | solution.py:18
  39.2 7.4 %all-to-all-start.4 = ((bf16[2,1,4,4096]{3,2,1,0:T(4,128)(2,1)}), bf16[2,1,4,4096]{3,2,1,0:T(4,128)(2,1)S(1)}, u32[]{:S(2)}, u32[]{:S(2)}) async-start(bf16[2,1,4,4096]{3,2,1,0:T(4,128)(2,1)} %bitcast.23), calls=%async_computation.4 | async-start | bytes 131072 | tf_op jit(solution)/shard_map/all_to_all | solution.py:71
  49.5 7.4 %all-to-all-start.2 = ((bf16[2,1,4,4096]{3,2,1,0:T(4,128)(2,1)}), bf16[2,1,4,4096]{3,2,1,0:T(4,128)(2,1)S(1)}, u32[]{:S(2)}, u32[]{:S(2)}) async-start(bf16[2,1,4,4096]{3,2,1,0:T(4,128)(2,1)} %bitcast.15), calls=%async_computation.2 | async-start | bytes 131072 | tf_op jit(solution)/shard_map/all_to_all | solution.py:30
  57.0 7.4 %all-to-all-start.5 = ((bf16[2,1,4,4096]{3,2,1,0:T(4,128)(2,1)}), bf16[2,1,4,4096]{3,2,1,0:T(4,128)(2,1)S(1)}, u32[]{:S(2)}, u32[]{:S(2)}) async-start(bf16[2,1,4,4096]{3,2,1,0:T(4,128)(2,1)} %bitcast.28), calls=%async_computation.5 | async-start | bytes 131072 | tf_op jit(solution)/shard_map/all_to_all | solution.py:30
where the time goes:
time: 66.6 us; the launch traced here: 65.8 us
  starting transfers between devices  29.2 us (44%)
  local copies, waits for them, and re-layouts  12.9 us (19%)
  waiting for transfers between devices  11.5 us (17%)
  blocking collectives  6.83 us (10%)
  other arithmetic  2.83 us (4%)
  matrix products  2.11 us (3%)
    ppermute x3, starting transfers between devices, from_behind(): return lax.ppermute(shard, axis, pairs)  11.7 us
    all_to_all x3, starting transfers between devices, on_device(): lax.all_to_all(for_sending(outgoing[turn]), 'srv', split_axis=0, concat_a...  10.9 us
    all_to_all x1, blocking collectives, on_device(): lax.all_to_all(for_sending(outgoing[turn]), 'srv', split_axis=0, concat_a...  6.83 us
    all_to_all x2, starting transfers between devices, give_back(): lax.all_to_all(served, 'srv', split_axis=0, concat_axis=0, tiled=True)  6.59 us
    all_to_all x2, waiting for transfers between devices, give_back(): lax.all_to_all(served, 'srv', split_axis=0, concat_axis=0, tiled=True)  5.26 us
    scatter x2, local copies, waits for them, and re-layouts, on_device(): sending = jnp.zeros((servers, 1, R, query_width), jnp.bfloat16).at[local_...  3.93 us
    all_to_all x3, waiting for transfers between devices, on_device(): lax.all_to_all(for_sending(outgoing[turn]), 'srv', split_axis=0, concat_a...  3.81 us
    ppermute x3, waiting for transfers between devices, from_behind(): return lax.ppermute(shard, axis, pairs)  2.43 us
  transfers between devices with their start and end apart: 8, of which 4 were waited for; matrix products, arithmetic and copies ran while one was open for 17% of the time, Pallas kernels for 0%

commit v1 on v0

v1 whole, which is shorter than its diff:
```python
import math

import jax
import jax.numpy as jnp
from jax import lax
from jax.experimental import pallas as pl
from jax.experimental.pallas import tpu as pltpu
from jax.sharding import PartitionSpec as P

QH = 32
KVH = 2
HD = 128
R = 4
ROUNDS = 2
BACK = 3
LANES = 128
MESH = pl.DeviceIdType.MESH


def each(count, body):
    if count <= 2:
        for index in range(count):
            body(index)
    else:
        lax.fori_loop(0, count, lambda index, carry: (body(index), carry)[1], 0)


def kernel(
    servers,
    blocks,
    destination,
    offsets,
    lengths,
    queries,
    key_rows,
    value_rows,
    out,
    own_queries,
    keys,
    values,
    query_out,
    query_in,
    place_out,
    place_in,
    scores,
    answers,
    returned,
    load_sem,
    kv_send,
    kv_recv,
    query_send,
    query_recv,
    place_send,
    place_recv,
    back_send,
    back_recv,
):
    me = lax.axis_index("srv")
    blk = lax.axis_index("blk")
    block_rows = key_rows.shape[1]
    tasks = destination.shape[2]
    per_round = tasks // ROUNDS
    groups = QH // KVH
    slot_rows = ROUNDS * R
    head_rows = groups * slot_rows
    scaling = 1.0 / math.sqrt(HD)
    docs = lengths.shape[1]

    load_queries = pltpu.make_async_copy(queries.at[0, 0], own_queries, load_sem.at[0])
    load_keys = pltpu.make_async_copy(
        key_rows.at[0], keys.at[pl.ds(0, block_rows)], load_sem.at[1]
    )
    load_values = pltpu.make_async_copy(
        value_rows.at[0], values.at[pl.ds(0, block_rows)], load_sem.at[2]
    )
    load_queries.start()
    load_keys.start()
    load_values.start()

    barrier = pltpu.get_barrier_semaphore()
    for hop in range(1, BACK + 1):

        @pl.when(blk + hop < blocks)
        def _():
            pl.semaphore_signal(
                barrier, inc=1, device_id={"blk": blk + hop}, device_id_type=MESH
            )

        @pl.when(blk >= hop)
        def _():
            pl.semaphore_signal(
                barrier, inc=1, device_id={"blk": blk - hop}, device_id_type=MESH
            )

    def greet(step):
        peer = lax.rem(me + 1 + step, servers)
        pl.semaphore_signal(barrier, inc=1, device_id={"srv": peer}, device_id_type=MESH)

    each(servers - 1, greet)

    for hop in range(1, BACK + 1):

        @pl.when(blk < hop)
        def _():
            empty = jnp.zeros((block_rows, keys.shape[1]), keys.dtype)
            keys[pl.ds(hop * block_rows, block_rows), :] = empty
            values[pl.ds(hop * block_rows, block_rows), :] = empty

    load_queries.wait()
    all_rows = own_queries[...]
    row = lax.broadcasted_iota(jnp.int32, (slot_rows, tasks * R), 0)
    column = lax.broadcasted_iota(jnp.int32, (slot_rows, tasks * R), 1)
    column_target = jnp.full((slot_rows, tasks * R), -1, jnp.int32)
    for task in range(tasks):
        column_target = jnp.where(
            column // R == task, destination[0, 0, task], column_target
        )
    same_place = (row // R == column // (per_round * R)) & (row % R == column % R)
    place_row = lax.broadcasted_iota(jnp.int32, (slot_rows, LANES), 0)

    def pack(slot):
        chosen = jnp.where(same_place & (column_target == slot), 1.0, 0.0).astype(jnp.bfloat16)
        routed = jnp.dot(chosen, all_rows, preferred_element_type=jnp.float32)
        for g in range(KVH):
            parts = [
                routed[:, (g * groups + h) * HD : (g * groups + h + 1) * HD]
                for h in range(groups)
            ]
            query_out[slot, g] = jnp.concatenate(parts, axis=0).astype(jnp.bfloat16)
        start = jnp.zeros((slot_rows, LANES), jnp.int32)
        for turn in range(ROUNDS):
            offset = jnp.int32(0)
            for t in range(per_round):
                task = turn * per_round + t
                offset = jnp.where(
                    destination[0, 0, task] == slot, offsets[0, 0, task], offset
                )
            start = jnp.where(place_row // R == turn, offset, start)
        place_out[slot] = start + place_row % R + blk * block_rows

    each(servers, pack)

    neighbours = (
        jnp.minimum(blk, BACK) + jnp.minimum(blocks - 1 - blk, BACK) + (servers - 1)
    )
    pl.semaphore_wait(barrier, neighbours)

    def query_copy(slot, source):
        return pltpu.make_async_remote_copy(
            src_ref=query_out.at[slot],
            dst_ref=query_in.at[source],
            send_sem=query_send.at[slot],
            recv_sem=query_recv.at[source],
            device_id={"srv": slot},
            device_id_type=MESH,
        )

    def place_copy(slot, source):
        return pltpu.make_async_remote_copy(
            src_ref=place_out.at[slot],
            dst_ref=place_in.at[source],
            send_sem=place_send.at[slot],
            recv_sem=place_recv.at[source],
            device_id={"srv": slot},
            device_id_type=MESH,
        )

    def back_copy(slot, g, server):
        return pltpu.make_async_remote_copy(
            src_ref=answers.at[slot, g],
            dst_ref=returned.at[server, g],
            send_sem=back_send.at[slot, g],
            recv_sem=back_recv.at[server, g],
            device_id={"srv": slot},
            device_id_type=MESH,
        )

    def kv_copy(hop, which):
        source, target = ((key_rows, keys), (value_rows, values))[which]
        return pltpu.make_async_remote_copy(
            src_ref=source.at[0],
            dst_ref=target.at[pl.ds(hop * block_rows, block_rows)],
            send_sem=kv_send.at[hop - 1, which],
            recv_sem=kv_recv.at[hop - 1, which],
            device_id={"blk": blk + hop},
            device_id_type=MESH,
        )

    def send_queries(step):
        peer = lax.rem(me + 1 + step, servers)
        query_copy(peer, me).start()
        place_copy(peer, me).start()

    each(servers - 1, send_queries)
    for which in range(2):
        for hop in range(BACK, 0, -1):

            @pl.when(blk + hop < blocks)
            def _():
                kv_copy(hop, which).start()

    query_in[me] = query_out[me]
    place_in[me] = place_out[me]
    load_keys.wait()

    def score(slot, hop):
        for g in range(KVH):
            block = keys[pl.ds(hop * block_rows, block_rows), g * HD : (g + 1) * HD]
            scores[slot, g, :, hop * block_rows : (hop + 1) * block_rows] = lax.dot_general(
                query_in[slot, g],
                block,
                (((1,), (1,)), ((), ())),
                preferred_element_type=jnp.float32,
            )

    score(me, 0)

    def first_scores(step):
        peer = lax.rem(me + 1 + step, servers)
        query_copy(peer, peer).wait_recv()
        place_copy(peer, peer).wait_recv()
        score(peer, 0)

    each(servers - 1, first_scores)
    for hop in range(1, BACK + 1):

        @pl.when(blk >= hop)
        def _():
            kv_copy(hop, 0).wait_recv()

        each(servers, lambda slot: score(slot, hop))
    load_values.wait()
    for hop in range(1, BACK + 1):

        @pl.when(blk >= hop)
        def _():
            kv_copy(hop, 1).wait_recv()

    ends = []
    running = jnp.int32(0)
    for doc in range(docs):
        running = running + lengths[0, doc]
        ends.append(running)
    lane = lax.broadcasted_iota(jnp.int32, (slot_rows, LANES), 1)

    def attend(slot, g):
        place = place_in[slot]
        first = jnp.zeros_like(place)
        for end in ends:
            first = jnp.where(end <= place, end, first)
        pieces = []
        highest = None
        for hop in range(BACK + 1):
            for part in range(block_rows // LANES):
                low = hop * block_rows + part * LANES
                at = (blk - hop) * block_rows + part * LANES + lane
                allowed = (at <= place) & (at >= first)
                piece = scores[slot, g, :, low : low + LANES] * scaling
                piece = piece.reshape(groups, slot_rows, LANES)
                piece = jnp.where(allowed[None], piece, -1e30)
                pieces.append(piece)
                highest = piece if highest is None else jnp.maximum(highest, piece)
        highest = jnp.max(highest, axis=2, keepdims=True)
        weights = [jnp.exp(piece - highest) for piece in pieces]
        total = weights[0]
        for weight in weights[1:]:
            total = total + weight
        total = jnp.sum(total, axis=2, keepdims=True)
        joined = jnp.concatenate(
            [w.reshape(head_rows, LANES).astype(jnp.bfloat16) for w in weights], axis=1
        )
        weighted = jnp.dot(
            joined, values[:, g * HD : (g + 1) * HD], preferred_element_type=jnp.float32
        )
        return (weighted / total.reshape(head_rows, 1)).astype(jnp.bfloat16)

    def serve(step):
        peer = lax.rem(me + 1 + step, servers)
        for g in range(KVH):
            answers[peer, g] = attend(peer, g)
            back_copy(peer, g, me).start()

    each(servers - 1, serve)
    for g in range(KVH):
        returned[me, g] = attend(me, g)

    def collect(step):
        peer = lax.rem(me + 1 + step, servers)
        for g in range(KVH):
            back_copy(peer, g, peer).wait_recv()

    each(servers - 1, collect)

    out_row = lax.broadcasted_iota(jnp.int32, (tasks * R, servers * slot_rows), 0)
    from_row = lax.broadcasted_iota(jnp.int32, (tasks * R, servers * slot_rows), 1)
    row_target = jnp.full((tasks * R, servers * slot_rows), -1, jnp.int32)
    for task in range(tasks):
        row_target = jnp.where(out_row // R == task, destination[0, 0, task], row_target)
    within = from_row % slot_rows
    taken = (
        (row_target == from_row // slot_rows)
        & (within // R == out_row // (per_round * R))
        & (within % R == out_row % R)
    )
    taken = jnp.where(taken, 1.0, 0.0).astype(jnp.bfloat16)
    for g in range(KVH):
        got = [returned[slot, g].astype(jnp.float32) for slot in range(servers)]
        wide = []
        for h in range(groups):
            stacked = [piece[h * slot_rows : (h + 1) * slot_rows] for piece in got]
            wide.append(jnp.concatenate(stacked, axis=0).astype(jnp.bfloat16))
        wide = jnp.concatenate(wide, axis=1)
        out[0, 0, :, g * groups * HD : (g + 1) * groups * HD] = jnp.dot(
            taken, wide, preferred_element_type=jnp.float32
        ).astype(jnp.bfloat16)

    def finish(step):
        peer = lax.rem(me + 1 + step, servers)
        query_copy(peer, me).wait_send()
        place_copy(peer, me).wait_send()
        for g in range(KVH):
            back_copy(peer, g, me).wait_send()

    each(servers - 1, finish)
    for which in range(2):
        for hop in range(1, BACK + 1):

            @pl.when(blk + hop < blocks)
            def _():
                kv_copy(hop, which).wait_send()


def solution(mesh):
    servers = mesh.shape["srv"]
    blocks = mesh.shape["blk"]
    placed = (
        P("srv", "blk", "rep", None),
        P("srv", "blk", "rep"),
        P("srv", "blk", "rep"),
        P("srv", "blk", "rep"),
        P("srv", "blk", "rep"),
        P("srv", "rep"),
    )

    def on_device(queries, destination, offsets, key_rows, value_rows, lengths):
        block_rows, kv_width = key_rows.shape[1:]
        slot_rows = ROUNDS * R
        packed = (servers, KVH, QH // KVH * slot_rows, HD)
        window = (BACK + 1) * block_rows
        smem = pl.BlockSpec(memory_space=pltpu.SMEM)
        anywhere = pl.BlockSpec(memory_space=pl.ANY)
        dma = pltpu.SemaphoreType.DMA

        def body(*refs):
            kernel(servers, blocks, *refs)

        return pl.pallas_call(
            body,
            name="routed_attention",
            out_shape=jax.ShapeDtypeStruct(queries.shape, queries.dtype),
            in_specs=[smem] * 3 + [anywhere] * 3,
            out_specs=pl.BlockSpec(memory_space=pltpu.VMEM),
            scratch_shapes=[
                pltpu.VMEM(queries.shape[2:], jnp.bfloat16),
                pltpu.VMEM((window, kv_width), jnp.bfloat16),
                pltpu.VMEM((window, kv_width), jnp.bfloat16),
                pltpu.VMEM(packed, jnp.bfloat16),
                pltpu.VMEM(packed, jnp.bfloat16),
                pltpu.VMEM((servers, slot_rows, LANES), jnp.int32),
                pltpu.VMEM((servers, slot_rows, LANES), jnp.int32),
                pltpu.VMEM(packed[:3] + (window,), jnp.float32),
                pltpu.VMEM(packed, jnp.bfloat16),
                pltpu.VMEM(packed, jnp.bfloat16),
                dma((3,)),
                dma((BACK, 2)),
                dma((BACK, 2)),
                dma((servers,)),
                dma((servers,)),
                dma((servers,)),
                dma((servers,)),
                dma((servers, KVH)),
                dma((servers, KVH)),
            ],
            compiler_params=pltpu.CompilerParams(collective_id=0, has_side_effects=True),
        )(destination, offsets, lengths, queries, key_rows, value_rows)

    return jax.shard_map(
        on_device,
        mesh=mesh,
        in_specs=placed,
        out_specs=P("srv", "blk", "rep", None),
        check_vma=False,
    )
```

time: 66.6 us -> 23.3 us (0.35)
  the two profiles are of different devices: /device:TPU:0 before, /device:TPU:16 now
where the time goes in v1:
time: 23.3 us; the launch traced here: 23.1 us
  Pallas kernels  21.6 us (93%)
  local copies, waits for them, and re-layouts  1.57 us (7%)
    pallas_call x1, Pallas kernels, on_device(): pl.pallas_call(body, name='routed_attention', out_shape=jax.ShapeDtypeStr...  21.6 us
    unnamed x1, local copies, waits for them, and re-layouts  1.57 us

profile of v1, /device:TPU:16, one launch (start us, length us, event | category | flops | bytes accessed | tf_op | source)
XLA Modules:
  0.0 23.1 jit_solution(15918073596193362103)
XLA Ops:
  0.0 21.6 %routed_attention.1 = bf16[1,1,16,4096]{3,2,1,0:T(8,128)(2,1)} custom-call(s32[1,1,4]{2,1,0:T(1,128)} %refs_0_.1, s32[1,1,4]{2,1,0:T(1,128)} %refs_1_.1, s32[1,8]{1,0:T(1,128)} %refs_2_.1, bf16[1,1,16,4096]{3,2,1,0:T(8,128)(2,1)} %refs_3_.1, bf16[1,128,256]{2,1,0:T(8,128)(2,1)} %refs_4_.1, bf16[1,128,256]{2,1,0:T(8,128)(2,1)} %refs_5_.1), custom_call_target="tpu_custom_call" | custom-call | tf_op jit(solution)/shard_map/routed_attention/pallas_call | solution.py:357
  21.6 1.6 %copy.8 = bf16[1,1,16,4096]{3,2,1,0:T(8,128)(2,1)} copy(bf16[1,1,16,4096]{3,2,1,0:T(8,128)(2,1)} %routed_attention.1) | data formatting | bytes 262144

commit v2 on v1

--- a/solution.py
+++ b/solution.py
@@ -13,6 +13,7 @@
 R = 4
 ROUNDS = 2
 BACK = 3
+CHUNKS = 4
 LANES = 128
 MESH = pl.DeviceIdType.MESH
 
@@ -46,7 +47,8 @@
     answers,
     returned,
     load_sem,
-    kv_send,
+    own_send,
+    relay_send,
     kv_recv,
     query_send,
     query_recv,
@@ -78,7 +80,7 @@
     load_values.start()
 
     barrier = pltpu.get_barrier_semaphore()
-    for hop in range(1, BACK + 1):
+    for hop in range(1, BACK):
 
         @pl.when(blk + hop < blocks)
         def _():
@@ -141,7 +143,9 @@
     each(servers, pack)
 
     neighbours = (
-        jnp.minimum(blk, BACK) + jnp.minimum(blocks - 1 - blk, BACK) + (servers - 1)
+        jnp.minimum(blk, BACK - 1)
+        + jnp.minimum(blocks - 1 - blk, BACK - 1)
+        + (servers - 1)
     )
     pl.semaphore_wait(barrier, neighbours)
 
@@ -175,16 +179,53 @@
             device_id_type=MESH,
         )
 
-    def kv_copy(hop, which):
-        source, target = ((key_rows, keys), (value_rows, values))[which]
+    half = block_rows // 2
+
+    def kv_copy(source, target, slot, hop, chunk, sent):
+        low = hop * block_rows + chunk % 2 * half
         return pltpu.make_async_remote_copy(
-            src_ref=source.at[0],
-            dst_ref=target.at[pl.ds(hop * block_rows, block_rows)],
-            send_sem=kv_send.at[hop - 1, which],
-            recv_sem=kv_recv.at[hop - 1, which],
-            device_id={"blk": blk + hop},
+            src_ref=source[chunk // 2].at[pl.ds(slot * block_rows + chunk % 2 * half, half)],
+            dst_ref=(keys, values)[chunk // 2].at[pl.ds(low, half)],
+            send_sem=sent.at[chunk],
+            recv_sem=kv_recv.at[hop - 1, chunk],
+            device_id={"blk": target},
             device_id_type=MESH,
         )
+
+    own = (key_rows.at[0], value_rows.at[0])
+    held = (keys, values)
+    is_odd = lax.rem(blk, 2) == 1
+    has_two = blk >= 2
+    by_relay = is_odd & (blk + 2 < blocks)
+    to_one = (blk + 1 < blocks) & jnp.logical_not(by_relay)
+
+    def own_one(chunk):
+        return kv_copy(own, blk + 1, 0, 1, chunk, own_send.at[0])
+
+    def own_two(chunk):
+        return kv_copy(own, blk + 2, 0, 2, chunk, own_send.at[1])
+
+    def relay_back(chunk):
+        return kv_copy(held, blk - 1, 2, 1, chunk, relay_send.at[0])
+
+    def relay_on(chunk):
+        return kv_copy(held, blk + 1, 2, 3, chunk, relay_send.at[1])
+
+    def arrived(hop, chunk):
+        return kv_copy(held, blk, 0, hop, chunk, own_send.at[0])
+
+    def pass_on(chunk):
+        @pl.when(has_two)
+        def _():
+            arrived(2, chunk).wait_recv()
+
+        @pl.when(has_two & (blk + 1 < blocks))
+        def _():
+            relay_on(chunk).start()
+
+        @pl.when(has_two & is_odd)
+        def _():
+            relay_back(chunk).start()
 
     def send_queries(step):
         peer = lax.rem(me + 1 + step, servers)
@@ -192,12 +233,15 @@
         place_copy(peer, me).start()
 
     each(servers - 1, send_queries)
-    for which in range(2):
-        for hop in range(BACK, 0, -1):
-
-            @pl.when(blk + hop < blocks)
-            def _():
-                kv_copy(hop, which).start()
+    for chunk in range(CHUNKS):
+
+        @pl.when(blk + 2 < blocks)
+        def _():
+            own_two(chunk).start()
+
+        @pl.when(to_one)
+        def _():
+            own_one(chunk).start()
 
     query_in[me] = query_out[me]
     place_in[me] = place_out[me]
@@ -214,6 +258,8 @@
             )
 
     score(me, 0)
+    pass_on(0)
+    pass_on(1)
 
     def first_scores(step):
         peer = lax.rem(me + 1 + step, servers)
@@ -222,19 +268,24 @@
         score(peer, 0)
 
     each(servers - 1, first_scores)
-    for hop in range(1, BACK + 1):
+    each(servers, lambda slot: score(slot, 2))
+    for chunk in range(CHUNKS // 2, CHUNKS):
+        pass_on(chunk)
+    for hop in (1, 3):
 
         @pl.when(blk >= hop)
         def _():
-            kv_copy(hop, 0).wait_recv()
+            for chunk in range(CHUNKS // 2):
+                arrived(hop, chunk).wait_recv()
 
         each(servers, lambda slot: score(slot, hop))
     load_values.wait()
-    for hop in range(1, BACK + 1):
+    for hop in (1, 3):
 
         @pl.when(blk >= hop)
         def _():
-            kv_copy(hop, 1).wait_recv()
+            for chunk in range(CHUNKS // 2, CHUNKS):
+                arrived(hop, chunk).wait_recv()
 
     ends = []
     running = jnp.int32(0)
@@ -322,12 +373,23 @@
             back_copy(peer, g, me).wait_send()
 
     each(servers - 1, finish)
-    for which in range(2):
-        for hop in range(1, BACK + 1):
-
-            @pl.when(blk + hop < blocks)
-            def _():
-                kv_copy(hop, which).wait_send()
+    for chunk in range(CHUNKS):
+
+        @pl.when(blk + 2 < blocks)
+        def _():
+            own_two(chunk).wait_send()
+
+        @pl.when(to_one)
+        def _():
+            own_one(chunk).wait_send()
+
+        @pl.when(has_two & (blk + 1 < blocks))
+        def _():
+            relay_on(chunk).wait_send()
+
+        @pl.when(has_two & is_odd)
+        def _():
+            relay_back(chunk).wait_send()
 
 
 def solution(mesh):
@@ -357,7 +419,7 @@
         return pl.pallas_call(
             body,
             name="routed_attention",
-            out_shape=jax.ShapeDtypeStruct(queries.shape, queries.dtype),
+            out_shape=pltpu.VMEM(queries.shape, queries.dtype),
             in_specs=[smem] * 3 + [anywhere] * 3,
             out_specs=pl.BlockSpec(memory_space=pltpu.VMEM),
             scratch_shapes=[
@@ -372,8 +434,9 @@
                 pltpu.VMEM(packed, jnp.bfloat16),
                 pltpu.VMEM(packed, jnp.bfloat16),
                 dma((3,)),
-                dma((BACK, 2)),
-                dma((BACK, 2)),
+                dma((2, CHUNKS)),
+                dma((2, CHUNKS)),
+                dma((BACK, CHUNKS)),
                 dma((servers,)),
                 dma((servers,)),
                 dma((servers,)),

time: 23.3 us -> 17 us (0.73)
  Pallas kernels: 21.6 us -> 16.1 us
  local copies, waits for them, and re-layouts: 1.57 us -> 0.66 us
    pallas_call x1, Pallas kernels: 21.6 us -> 16.1 us  [on_device(): pl.pallas_call(body, name='routed_attention', out_shape=pltpu.VMEM(querie...]
    unnamed x1, local copies, waits for them, and re-layouts: 1.57 us -> 0.66 us
where the time goes in v2:
time: 17 us; the launch traced here: 16.8 us
  Pallas kernels  16.1 us (95%)
  local copies, waits for them, and re-layouts  0.66 us (4%)
    pallas_call x1, Pallas kernels, on_device(): pl.pallas_call(body, name='routed_attention', out_shape=pltpu.VMEM(querie...  16.1 us
    unnamed x1, local copies, waits for them, and re-layouts  0.66 us

profile of v2, /device:TPU:16, one launch (start us, length us, event | category | flops | bytes accessed | tf_op | source)
XLA Modules:
  0.0 16.8 jit_solution(10682340406323809055)
XLA Ops:
  0.0 16.1 %routed_attention.1 = bf16[1,1,16,4096]{3,2,1,0:T(8,128)(2,1)S(1)} custom-call(s32[1,1,4]{2,1,0:T(1,128)} %refs_0_.1, s32[1,1,4]{2,1,0:T(1,128)} %refs_1_.1, s32[1,8]{1,0:T(1,128)} %refs_2_.1, bf16[1,1,16,4096]{3,2,1,0:T(8,128)(2,1)} %refs_3_.1, bf16[1,128,256]{2,1,0:T(8,128)(2,1)} %refs_4_.1, bf16[1,128,256]{2,1,0:T(8,128)(2,1)} %refs_5_.1), custom_call_target="tpu_custom_call" | custom-call | tf_op jit(solution)/shard_map/routed_attention/pallas_call | solution.py:419
  16.2 0.7 %copy.8 = bf16[1,1,16,4096]{3,2,1,0:T(8,128)(2,1)} copy(bf16[1,1,16,4096]{3,2,1,0:T(8,128)(2,1)S(1)} %routed_attention.1) | data formatting | bytes 262144

commit v3 on v2

--- a/solution.py
+++ b/solution.py
@@ -44,6 +44,8 @@
     place_out,
     place_in,
     scores,
+    weights,
+    totals,
     answers,
     returned,
     load_sem,
@@ -179,13 +181,15 @@
             device_id_type=MESH,
         )
 
-    half = block_rows // 2
+    pieces = CHUNKS // 2
+    part_rows = block_rows // pieces
 
     def kv_copy(source, target, slot, hop, chunk, sent):
-        low = hop * block_rows + chunk % 2 * half
+        part = chunk % pieces * part_rows
+        low = hop * block_rows + part
         return pltpu.make_async_remote_copy(
-            src_ref=source[chunk // 2].at[pl.ds(slot * block_rows + chunk % 2 * half, half)],
-            dst_ref=(keys, values)[chunk // 2].at[pl.ds(low, half)],
+            src_ref=source[chunk // pieces].at[pl.ds(slot * block_rows + part, part_rows)],
+            dst_ref=(keys, values)[chunk // pieces].at[pl.ds(low, part_rows)],
             send_sem=sent.at[chunk],
             recv_sem=kv_recv.at[hop - 1, chunk],
             device_id={"blk": target},
@@ -195,9 +199,9 @@
     own = (key_rows.at[0], value_rows.at[0])
     held = (keys, values)
     is_odd = lax.rem(blk, 2) == 1
-    has_two = blk >= 2
-    by_relay = is_odd & (blk + 2 < blocks)
-    to_one = (blk + 1 < blocks) & jnp.logical_not(by_relay)
+    relays = (blk >= 2) & jnp.logical_not(is_odd)
+    has_one = blk + 1 < blocks
+    has_next = blk + 2 < blocks
 
     def own_one(chunk):
         return kv_copy(own, blk + 1, 0, 1, chunk, own_send.at[0])
@@ -205,27 +209,32 @@
     def own_two(chunk):
         return kv_copy(own, blk + 2, 0, 2, chunk, own_send.at[1])
 
-    def relay_back(chunk):
-        return kv_copy(held, blk - 1, 2, 1, chunk, relay_send.at[0])
-
     def relay_on(chunk):
-        return kv_copy(held, blk + 1, 2, 3, chunk, relay_send.at[1])
+        return kv_copy(held, blk + 1, 2, 3, chunk, relay_send.at[0])
 
     def arrived(hop, chunk):
         return kv_copy(held, blk, 0, hop, chunk, own_send.at[0])
 
-    def pass_on(chunk):
-        @pl.when(has_two)
-        def _():
-            arrived(2, chunk).wait_recv()
-
-        @pl.when(has_two & (blk + 1 < blocks))
+    def relay_two(chunk):
+        return kv_copy(held, blk + 2, 1, 3, chunk, relay_send.at[1])
+
+    def await_all(hop, chunks):
+        for chunk in chunks:
+            arrived(hop, chunk).wait_recv()
+
+    def take_two(chunk):
+        arrived(2, chunk).wait_recv()
+
+        @pl.when(has_one)
         def _():
             relay_on(chunk).start()
 
-        @pl.when(has_two & is_odd)
+    def take_one(chunk):
+        arrived(1, chunk).wait_recv()
+
+        @pl.when(has_next)
         def _():
-            relay_back(chunk).start()
+            relay_two(chunk).start()
 
     def send_queries(step):
         peer = lax.rem(me + 1 + step, servers)
@@ -233,15 +242,15 @@
         place_copy(peer, me).start()
 
     each(servers - 1, send_queries)
-    for chunk in range(CHUNKS):
-
-        @pl.when(blk + 2 < blocks)
-        def _():
+    @pl.when(has_one)
+    def _():
+        for chunk in range(CHUNKS):
+            own_one(chunk).start()
+
+    @pl.when(has_next)
+    def _():
+        for chunk in range(CHUNKS):
             own_two(chunk).start()
-
-        @pl.when(to_one)
-        def _():
-            own_one(chunk).start()
 
     query_in[me] = query_out[me]
     place_in[me] = place_out[me]
@@ -258,8 +267,13 @@
             )
 
     score(me, 0)
-    pass_on(0)
-    pass_on(1)
+    @pl.when(relays)
+    def _():
+        take_two(0)
+        for chunk in range(CHUNKS):
+            if chunk + 1 < CHUNKS:
+                take_two(chunk + 1)
+            take_one(chunk)
 
     def first_scores(step):
         peer = lax.rem(me + 1 + step, servers)
@@ -268,24 +282,25 @@
         score(peer, 0)
 
     each(servers - 1, first_scores)
+    first_half, second_half = range(pieces), range(pieces, CHUNKS)
+
+    @pl.when(is_odd)
+    def _():
+        await_all(1, first_half)
+
+    each(servers, lambda slot: score(slot, 1))
+
+    @pl.when(is_odd & (blk >= 2))
+    def _():
+        await_all(2, first_half)
+
     each(servers, lambda slot: score(slot, 2))
-    for chunk in range(CHUNKS // 2, CHUNKS):
-        pass_on(chunk)
-    for hop in (1, 3):
-
-        @pl.when(blk >= hop)
-        def _():
-            for chunk in range(CHUNKS // 2):
-                arrived(hop, chunk).wait_recv()
-
-        each(servers, lambda slot: score(slot, hop))
-    load_values.wait()
-    for hop in (1, 3):
-
-        @pl.when(blk >= hop)
-        def _():
-            for chunk in range(CHUNKS // 2, CHUNKS):
-                arrived(hop, chunk).wait_recv()
+
+    @pl.when(blk >= 3)
+    def _():
+        await_all(3, first_half)
+
+    each(servers, lambda slot: score(slot, 3))
 
     ends = []
     running = jnp.int32(0)
@@ -294,36 +309,56 @@
         ends.append(running)
     lane = lax.broadcasted_iota(jnp.int32, (slot_rows, LANES), 1)
 
-    def attend(slot, g):
+    def weigh(slot):
         place = place_in[slot]
         first = jnp.zeros_like(place)
         for end in ends:
             first = jnp.where(end <= place, end, first)
-        pieces = []
-        highest = None
-        for hop in range(BACK + 1):
-            for part in range(block_rows // LANES):
-                low = hop * block_rows + part * LANES
-                at = (blk - hop) * block_rows + part * LANES + lane
+        for g in range(KVH):
+            logits = []
+            highest = None
+            for low in range(0, (BACK + 1) * block_rows, LANES):
+                hop = low // block_rows
+                at = (blk - hop) * block_rows + low % block_rows + lane
                 allowed = (at <= place) & (at >= first)
                 piece = scores[slot, g, :, low : low + LANES] * scaling
                 piece = piece.reshape(groups, slot_rows, LANES)
                 piece = jnp.where(allowed[None], piece, -1e30)
-                pieces.append(piece)
+                logits.append(piece)
                 highest = piece if highest is None else jnp.maximum(highest, piece)
-        highest = jnp.max(highest, axis=2, keepdims=True)
-        weights = [jnp.exp(piece - highest) for piece in pieces]
-        total = weights[0]
-        for weight in weights[1:]:
-            total = total + weight
-        total = jnp.sum(total, axis=2, keepdims=True)
-        joined = jnp.concatenate(
-            [w.reshape(head_rows, LANES).astype(jnp.bfloat16) for w in weights], axis=1
-        )
+            highest = jnp.max(highest, axis=2, keepdims=True)
+            total = None
+            for index, piece in enumerate(logits):
+                weight = jnp.exp(piece - highest)
+                total = weight if total is None else total + weight
+                weights[slot, g, :, index * LANES : (index + 1) * LANES] = weight.reshape(
+                    head_rows, LANES
+                ).astype(jnp.bfloat16)
+            total = jnp.sum(total, axis=2, keepdims=True).reshape(head_rows, 1)
+            totals[slot, g] = jnp.broadcast_to(total, (head_rows, HD))
+
+    def attend(slot, g):
         weighted = jnp.dot(
-            joined, values[:, g * HD : (g + 1) * HD], preferred_element_type=jnp.float32
-        )
-        return (weighted / total.reshape(head_rows, 1)).astype(jnp.bfloat16)
+            weights[slot, g],
+            values[:, g * HD : (g + 1) * HD],
+            preferred_element_type=jnp.float32,
+        )
+        return (weighted / totals[slot, g]).astype(jnp.bfloat16)
+
+    each(servers, weigh)
+    load_values.wait()
+
+    @pl.when(is_odd)
+    def _():
+        await_all(1, second_half)
+
+    @pl.when(is_odd & (blk >= 2))
+    def _():
+        await_all(2, second_half)
+
+    @pl.when(blk >= 3)
+    def _():
+        await_all(3, second_half)
 
     def serve(step):
         peer = lax.rem(me + 1 + step, servers)
@@ -373,23 +408,25 @@
             back_copy(peer, g, me).wait_send()
 
     each(servers - 1, finish)
-    for chunk in range(CHUNKS):
-
-        @pl.when(blk + 2 < blocks)
-        def _():
+    @pl.when(has_one)
+    def _():
+        for chunk in range(CHUNKS):
+            own_one(chunk).wait_send()
+
+    @pl.when(has_next)
+    def _():
+        for chunk in range(CHUNKS):
             own_two(chunk).wait_send()
 
-        @pl.when(to_one)
-        def _():
-            own_one(chunk).wait_send()
-
-        @pl.when(has_two & (blk + 1 < blocks))
-        def _():
+    @pl.when(relays & has_one)
+    def _():
+        for chunk in range(CHUNKS):
             relay_on(chunk).wait_send()
 
-        @pl.when(has_two & is_odd)
-        def _():
-            relay_back(chunk).wait_send()
+    @pl.when(relays & has_next)
+    def _():
+        for chunk in range(CHUNKS):
+            relay_two(chunk).wait_send()
 
 
 def solution(mesh):
@@ -431,6 +468,8 @@
                 pltpu.VMEM((servers, slot_rows, LANES), jnp.int32),
                 pltpu.VMEM((servers, slot_rows, LANES), jnp.int32),
                 pltpu.VMEM(packed[:3] + (window,), jnp.float32),
+                pltpu.VMEM(packed[:3] + (window,), jnp.bfloat16),
+                pltpu.VMEM(packed, jnp.float32),
                 pltpu.VMEM(packed, jnp.bfloat16),
                 pltpu.VMEM(packed, jnp.bfloat16),
                 dma((3,)),

time: 17 us -> 16 us (0.941)
  Pallas kernels: 16.1 us -> 15.1 us
    pallas_call x1, Pallas kernels: 16.1 us -> 15.1 us  [on_device(): pl.pallas_call(body, name='routed_attention', out_shape=pltpu.VMEM(querie...]
where the time goes in v3:
time: 16 us; the launch traced here: 15.8 us
  Pallas kernels  15.1 us (94%)
  local copies, waits for them, and re-layouts  0.66 us (4%)
    pallas_call x1, Pallas kernels, on_device(): pl.pallas_call(body, name='routed_attention', out_shape=pltpu.VMEM(querie...  15.1 us
    unnamed x1, local copies, waits for them, and re-layouts  0.66 us

profile of v3, /device:TPU:16, one launch (start us, length us, event | category | flops | bytes accessed | tf_op | source)
XLA Modules:
  0.0 15.8 jit_solution(10775083367478773482)
XLA Ops:
  0.0 15.1 %routed_attention.1 = bf16[1,1,16,4096]{3,2,1,0:T(8,128)(2,1)S(1)} custom-call(s32[1,1,4]{2,1,0:T(1,128)} %refs_0_.1, s32[1,1,4]{2,1,0:T(1,128)} %refs_1_.1, s32[1,8]{1,0:T(1,128)} %refs_2_.1, bf16[1,1,16,4096]{3,2,1,0:T(8,128)(2,1)} %refs_3_.1, bf16[1,128,256]{2,1,0:T(8,128)(2,1)} %refs_4_.1, bf16[1,128,256]{2,1,0:T(8,128)(2,1)} %refs_5_.1), custom_call_target="tpu_custom_call" | custom-call | tf_op jit(solution)/shard_map/routed_attention/pallas_call | solution.py:456
  15.1 0.7 %copy.8 = bf16[1,1,16,4096]{3,2,1,0:T(8,128)(2,1)} copy(bf16[1,1,16,4096]{3,2,1,0:T(8,128)(2,1)S(1)} %routed_attention.1) | data formatting | bytes 262144

commit v4 on v3

--- a/solution.py
+++ b/solution.py
@@ -46,6 +46,7 @@
     scores,
     weights,
     totals,
+    gathered,
     answers,
     returned,
     load_sem,
@@ -200,6 +201,7 @@
     held = (keys, values)
     is_odd = lax.rem(blk, 2) == 1
     relays = (blk >= 2) & jnp.logical_not(is_odd)
+    late = is_odd & (lax.axis_index("rep") == 1)
     has_one = blk + 1 < blocks
     has_next = blk + 2 < blocks
 
@@ -247,7 +249,7 @@
         for chunk in range(CHUNKS):
             own_one(chunk).start()
 
-    @pl.when(has_next)
+    @pl.when(has_next & jnp.logical_not(late))
     def _():
         for chunk in range(CHUNKS):
             own_two(chunk).start()
@@ -267,6 +269,21 @@
             )
 
     score(me, 0)
+    first_half, second_half = range(pieces), range(pieces, CHUNKS)
+
+    @pl.when(is_odd)
+    def _():
+        await_all(1, first_half)
+
+    @pl.when(late)
+    def _():
+        await_all(1, second_half)
+
+    @pl.when(has_next & late)
+    def _():
+        for chunk in range(CHUNKS):
+            own_two(chunk).start()
+
     @pl.when(relays)
     def _():
         take_two(0)
@@ -282,12 +299,6 @@
         score(peer, 0)
 
     each(servers - 1, first_scores)
-    first_half, second_half = range(pieces), range(pieces, CHUNKS)
-
-    @pl.when(is_odd)
-    def _():
-        await_all(1, first_half)
-
     each(servers, lambda slot: score(slot, 1))
 
     @pl.when(is_odd & (blk >= 2))
@@ -348,7 +359,7 @@
     each(servers, weigh)
     load_values.wait()
 
-    @pl.when(is_odd)
+    @pl.when(is_odd & jnp.logical_not(late))
     def _():
         await_all(1, second_half)
 
@@ -370,35 +381,32 @@
     for g in range(KVH):
         returned[me, g] = attend(me, g)
 
+    out_row = lax.broadcasted_iota(jnp.int32, (tasks * R, slot_rows), 0)
+    from_row = lax.broadcasted_iota(jnp.int32, (tasks * R, slot_rows), 1)
+    row_target = jnp.full((tasks * R, slot_rows), -1, jnp.int32)
+    for task in range(tasks):
+        row_target = jnp.where(out_row // R == task, destination[0, 0, task], row_target)
+    aligned = (from_row // R == out_row // (per_round * R)) & (from_row % R == out_row % R)
+
+    def unpack(slot, g):
+        taken = jnp.where(aligned & (row_target == slot), 1.0, 0.0).astype(jnp.bfloat16)
+        got = returned[slot, g].astype(jnp.float32)
+        wide = [got[h * slot_rows : (h + 1) * slot_rows] for h in range(groups)]
+        wide = jnp.concatenate(wide, axis=1).astype(jnp.bfloat16)
+        return jnp.dot(taken, wide, preferred_element_type=jnp.float32)
+
+    for g in range(KVH):
+        gathered[g] = unpack(me, g)
+
     def collect(step):
         peer = lax.rem(me + 1 + step, servers)
         for g in range(KVH):
             back_copy(peer, g, peer).wait_recv()
+            gathered[g] += unpack(peer, g)
 
     each(servers - 1, collect)
-
-    out_row = lax.broadcasted_iota(jnp.int32, (tasks * R, servers * slot_rows), 0)
-    from_row = lax.broadcasted_iota(jnp.int32, (tasks * R, servers * slot_rows), 1)
-    row_target = jnp.full((tasks * R, servers * slot_rows), -1, jnp.int32)
-    for task in range(tasks):
-        row_target = jnp.where(out_row // R == task, destination[0, 0, task], row_target)
-    within = from_row % slot_rows
-    taken = (
-        (row_target == from_row // slot_rows)
-        & (within // R == out_row // (per_round * R))
-        & (within % R == out_row % R)
-    )
-    taken = jnp.where(taken, 1.0, 0.0).astype(jnp.bfloat16)
     for g in range(KVH):
-        got = [returned[slot, g].astype(jnp.float32) for slot in range(servers)]
-        wide = []
-        for h in range(groups):
-            stacked = [piece[h * slot_rows : (h + 1) * slot_rows] for piece in got]
-            wide.append(jnp.concatenate(stacked, axis=0).astype(jnp.bfloat16))
-        wide = jnp.concatenate(wide, axis=1)
-        out[0, 0, :, g * groups * HD : (g + 1) * groups * HD] = jnp.dot(
-            taken, wide, preferred_element_type=jnp.float32
-        ).astype(jnp.bfloat16)
+        out[0, 0, :, g * groups * HD : (g + 1) * groups * HD] = gathered[g].astype(jnp.bfloat16)
 
     def finish(step):
         peer = lax.rem(me + 1 + step, servers)
@@ -470,6 +478,7 @@
                 pltpu.VMEM(packed[:3] + (window,), jnp.float32),
                 pltpu.VMEM(packed[:3] + (window,), jnp.bfloat16),
                 pltpu.VMEM(packed, jnp.float32),
+                pltpu.VMEM((KVH, queries.shape[2], QH // KVH * HD), jnp.float32),
                 pltpu.VMEM(packed, jnp.bfloat16),
                 pltpu.VMEM(packed, jnp.bfloat16),
                 dma((3,)),

time: 16 us -> 14.8 us (0.925)
  Pallas kernels: 15.1 us -> 14 us
    pallas_call x1, Pallas kernels: 15.1 us -> 14 us  [on_device(): pl.pallas_call(body, name='routed_attention', out_shape=pltpu.VMEM(querie...]
where the time goes in v4:
time: 14.8 us; the launch traced here: 14.6 us
  Pallas kernels  14 us (95%)
  local copies, waits for them, and re-layouts  0.66 us (4%)
    pallas_call x1, Pallas kernels, on_device(): pl.pallas_call(body, name='routed_attention', out_shape=pltpu.VMEM(querie...  14 us
    unnamed x1, local copies, waits for them, and re-layouts  0.66 us

profile of v4, /device:TPU:16, one launch (start us, length us, event | category | flops | bytes accessed | tf_op | source)
XLA Modules:
  0.0 14.6 jit_solution(1035079825684155792)
XLA Ops:
  0.0 14.0 %routed_attention.1 = bf16[1,1,16,4096]{3,2,1,0:T(8,128)(2,1)S(1)} custom-call(s32[1,1,4]{2,1,0:T(1,128)} %refs_0_.1, s32[1,1,4]{2,1,0:T(1,128)} %refs_1_.1, s32[1,8]{1,0:T(1,128)} %refs_2_.1, bf16[1,1,16,4096]{3,2,1,0:T(8,128)(2,1)} %refs_3_.1, bf16[1,128,256]{2,1,0:T(8,128)(2,1)} %refs_4_.1, bf16[1,128,256]{2,1,0:T(8,128)(2,1)} %refs_5_.1), custom_call_target="tpu_custom_call" | custom-call | tf_op jit(solution)/shard_map/routed_attention/pallas_call | solution.py:464
  14.0 0.7 %copy.8 = bf16[1,1,16,4096]{3,2,1,0:T(8,128)(2,1)} copy(bf16[1,1,16,4096]{3,2,1,0:T(8,128)(2,1)S(1)} %routed_attention.1) | data formatting | bytes 262144

commit v5 on v4

--- a/solution.py
+++ b/solution.py
@@ -286,11 +286,9 @@
 
     @pl.when(relays)
     def _():
-        take_two(0)
-        for chunk in range(CHUNKS):
-            if chunk + 1 < CHUNKS:
-                take_two(chunk + 1)
+        for chunk in range(CHUNKS):
             take_one(chunk)
+            take_two(chunk)
 
     def first_scores(step):
         peer = lax.rem(me + 1 + step, servers)

time: 14.8 us -> 14.9 us (level)
  no operation moved by 1% of the time
where the time goes in v5:
time: 14.9 us; the launch traced here: 14.6 us
  Pallas kernels  14 us (94%)
  local copies, waits for them, and re-layouts  0.66 us (4%)
    pallas_call x1, Pallas kernels, on_device(): pl.pallas_call(body, name='routed_attention', out_shape=pltpu.VMEM(querie...  14 us
    unnamed x1, local copies, waits for them, and re-layouts  0.66 us

profile of v5, /device:TPU:16, one launch (start us, length us, event | category | flops | bytes accessed | tf_op | source)
XLA Modules:
  0.0 14.6 jit_solution(1138886198121096449)
XLA Ops:
  0.0 14.0 %routed_attention.1 = bf16[1,1,16,4096]{3,2,1,0:T(8,128)(2,1)S(1)} custom-call(s32[1,1,4]{2,1,0:T(1,128)} %refs_0_.1, s32[1,1,4]{2,1,0:T(1,128)} %refs_1_.1, s32[1,8]{1,0:T(1,128)} %refs_2_.1, bf16[1,1,16,4096]{3,2,1,0:T(8,128)(2,1)} %refs_3_.1, bf16[1,128,256]{2,1,0:T(8,128)(2,1)} %refs_4_.1, bf16[1,128,256]{2,1,0:T(8,128)(2,1)} %refs_5_.1), custom_call_target="tpu_custom_call" | custom-call | tf_op jit(solution)/shard_map/routed_attention/pallas_call | solution.py:462
  14.0 0.7 %copy.8 = bf16[1,1,16,4096]{3,2,1,0:T(8,128)(2,1)} copy(bf16[1,1,16,4096]{3,2,1,0:T(8,128)(2,1)S(1)} %routed_attention.1) | data formatting | bytes 262144
